TPU v7x, 32 devices: a whole 2x2x4 slice. The times are simulated.
32 devices in a mesh: dp: 8 (over y, x, core), mp: 4 (over z).
Axes of the slice: x: 2, y: 2, z: 4, core: 2. Of those that a mesh axis runs over, the one named last changes fastest.
Arguments:
- tokens: bfloat16 [64, 256, 1024], P(('dp', 'mp')), may hold values from -6 to 6
- cotangent: bfloat16 [64, 256, 1024], P(('dp', 'mp')), may hold values from -6 to 6
- w_qkv: bfloat16 [3, 1024, 1024], P(None, None, 'mp'), may hold values from -0.1875 to 0.1875
- w_out: bfloat16 [1024, 1024], P('mp'), may hold values from -1 to 1
- w_up: bfloat16 [1024, 4096], P(None, 'mp'), may hold values from -0.1875 to 0.1875
- w_down: bfloat16 [4096, 1024], P('mp'), may hold values from -0.09375 to 0.09375
- w_mod: bfloat16 [1024, 6144], P('mp'), may hold values from -0.1875 to 0.1875
- b_mod: bfloat16 [6, 1024], replicated, may hold values from -3 to 3
- time_weight: bfloat16 [256, 1024], P(None, 'mp'), may hold values from -0.375 to 0.375
- class_table: bfloat16 [1000, 1024], P(None, 'mp'), may hold values from -6 to 6
- rel_table: bfloat16 [16, 961], P('mp'), may hold values from -5 to 5
- window_step: int32 [64], P('dp'), may hold values from 0 to 999
- window_label: int32 [64], P('dp'), may hold values from 0 to 999
- window_cols: int32 [64], P('dp'), may hold values from 0 to 16, as said below
Outputs:
- block_out: bfloat16 [64, 256, 1024], P(('dp', 'mp'))
- tokens_grad: bfloat16 [64, 256, 1024], P(('dp', 'mp'))
- w_qkv_grad: float32 [3, 1024, 1024], P(None, None, 'mp')
- w_out_grad: float32 [1024, 1024], P('mp')
- w_up_grad: float32 [1024, 4096], P(None, 'mp')
- w_down_grad: float32 [4096, 1024], P('mp')
- w_mod_grad: float32 [1024, 6144], P('mp')
- b_mod_grad: float32 [6, 1024], replicated
- time_weight_grad: float32 [256, 1024], P(None, 'mp')
- class_table_grad: float32 [1000, 1024], P(None, 'mp')
- rel_table_grad: float32 [16, 961], P('mp')
Inputs may be any that keep to these rules, and one draw needn't show every extreme that they name: `window_cols`: within each aligned block of 8 windows the used slots (nonzero entry) come first, two or more of them; some block is used in full. A used slot holds 16 or 8 valid columns, an unused one 0.
All inputs are finite; a program needn't handle non-finite values.
Results may differ from a plain program's by a relative error of at most 0.028.
Values may be sent and summed in bfloat16 or wider, within the bound.
No kernel may reach another device: no remote copies, remote signals or barrier semaphores. Data moves between devices by JAX's collectives and lax.ppermute only.
A program may use at most 192 MiB of HBM per device.

v0:
```python
import math
import jax
import jax.numpy as jnp
from jax import lax
from jax.sharding import PartitionSpec as P

HEAD_DIM = 64
WSIDE = 16
FREQ = 256
EPS = 1e-06
HIGH = lax.Precision.HIGHEST
MASKED = -1000000000.0


def exact(matrix_a, matrix_b):
    return jnp.dot(matrix_a, matrix_b, precision=HIGH, preferred_element_type=jnp.float32)


def layer_norm(field):
    center = field - jnp.mean(field, axis=-1, keepdims=True)
    spread = jnp.mean(center * center, axis=-1, keepdims=True)
    return center * lax.rsqrt(spread + EPS)


def modulate(field, scale_part, shift_part):
    return layer_norm(field) * (1.0 + scale_part) + shift_part


def gelu_tanh(field):
    return jax.nn.gelu(field, approximate=True)


def step_features(step_ids, half_width):
    frequency = jnp.exp(-math.log(10000.0) * jnp.arange(half_width, dtype=jnp.float32) / half_width)
    angles = step_ids.astype(jnp.float32)[:, None] * frequency[None, :]
    return jnp.concatenate([jnp.cos(angles), jnp.sin(angles)], axis=1)


def offset_table(window_side):
    offsets = jnp.arange(window_side, dtype=jnp.int32)
    offset_diff = offsets[:, None] - offsets[None, :] + window_side - 1
    return (
        offset_diff[None] == jnp.arange(2 * window_side - 1, dtype=jnp.int32)[:, None, None]
    ).astype(jnp.float32)


def make_scores(queries, keys, rel_bias, keep_keys, score_scale):
    raw_scores = (
        jnp.einsum("wihd,wjhd->whij", queries, keys, preferred_element_type=jnp.float32)
        * score_scale
        + rel_bias[None]
    )
    return jnp.where(keep_keys[:, None, None, :], raw_scores, MASKED)


def per_device(
    tokens,
    cotangent,
    w_qkv,
    w_out,
    w_up,
    w_down,
    w_mod,
    b_mod,
    time_weight,
    class_table,
    rel_table,
    window_step,
    window_label,
    window_cols,
):
    own_count, win_tok, width = tokens.shape
    group_size = window_step.shape[0]
    local_heads = w_out.shape[0] // HEAD_DIM
    score_scale = HEAD_DIM ** (-0.5)
    first_own = lax.axis_index("mp") * own_count
    features = step_features(window_step, FREQ // 2).astype(jnp.bfloat16)
    classes = jnp.arange(class_table.shape[0], dtype=jnp.int32)
    onehot = (window_label[:, None] == classes[None, :]).astype(jnp.bfloat16)
    cond_pre = jnp.dot(features, time_weight, preferred_element_type=jnp.float32) + jnp.dot(
        onehot, class_table, preferred_element_type=jnp.float32
    )
    condition = jax.nn.silu(cond_pre).astype(jnp.bfloat16)
    partial_mod = jnp.dot(condition, w_mod, preferred_element_type=jnp.float32)
    modulation = (
        lax.psum(partial_mod, "mp").reshape(group_size, 6, width) + b_mod.astype(jnp.float32)[None]
    )
    own_mod = lax.dynamic_slice_in_dim(modulation, first_own, own_count, 0)
    shift_attn, scale_attn, gate_attn, shift_mlp, scale_mlp, gate_mlp = [
        own_mod[:, column][:, None, :] for column in range(6)
    ]
    token_cols = jnp.arange(win_tok, dtype=jnp.int32) % WSIDE
    keep_keys = token_cols[None, :] < window_cols[:, None]
    keep_rows = lax.dynamic_slice_in_dim(keep_keys, first_own, own_count, 0)[:, :, None]
    rel_span = 2 * WSIDE - 1
    offset_pick = offset_table(WSIDE)
    rel_grid = rel_table.astype(jnp.float32).reshape(local_heads, rel_span, rel_span)
    half_bias = jnp.einsum("ayz,hab->hyzb", offset_pick, rel_grid, precision=HIGH)
    rel_bias = jnp.einsum("hyzb,bxw->hyxzw", half_bias, offset_pick, precision=HIGH).reshape(
        local_heads, win_tok, win_tok
    )
    inputs = tokens.astype(jnp.float32)
    normed_attn = modulate(inputs, scale_attn, shift_attn).astype(jnp.bfloat16)
    gathered_attn = lax.all_gather(normed_attn, "mp", axis=0, tiled=True)
    projected = jnp.einsum(
        "wtd,kde->kwte", gathered_attn, w_qkv, preferred_element_type=jnp.float32
    ).astype(jnp.bfloat16)
    split_shape = (group_size, win_tok, local_heads, HEAD_DIM)
    queries = projected[0].reshape(split_shape)
    keys = projected[1].reshape(split_shape)
    values = projected[2].reshape(split_shape)
    scores = make_scores(queries, keys, rel_bias, keep_keys, score_scale)
    row_max = jnp.max(scores, axis=-1, keepdims=True)
    log_total = row_max + jnp.log(jnp.sum(jnp.exp(scores - row_max), axis=-1, keepdims=True))
    probs_low = jnp.exp(scores - log_total).astype(jnp.bfloat16)
    attended = (
        jnp.einsum("whij,wjhd->wihd", probs_low, values, preferred_element_type=jnp.float32)
        .astype(jnp.bfloat16)
        .reshape(group_size, win_tok, local_heads * HEAD_DIM)
    )
    row_block = attended
    branch = lax.psum_scatter(
        jnp.einsum("wte,ed->wtd", row_block, w_out, preferred_element_type=jnp.float32).astype(
            jnp.bfloat16
        ),
        "mp",
        scatter_dimension=0,
        tiled=True,
    ).astype(jnp.float32)
    middle = inputs + gate_attn * branch
    normed_mlp = modulate(middle, scale_mlp, shift_mlp).astype(jnp.bfloat16)
    gathered_mlp = lax.all_gather(normed_mlp, "mp", axis=0, tiled=True)
    hidden_pre = jnp.einsum("wtd,df->wtf", gathered_mlp, w_up, preferred_element_type=jnp.float32)
    activation = gelu_tanh(hidden_pre).astype(jnp.bfloat16)
    row_block = activation
    mlp_out = lax.psum_scatter(
        jnp.einsum("wtf,fd->wtd", row_block, w_down, preferred_element_type=jnp.float32).astype(
            jnp.bfloat16
        ),
        "mp",
        scatter_dimension=0,
        tiled=True,
    ).astype(jnp.float32)
    block_out = jnp.where(keep_rows, middle + gate_mlp * mlp_out, 0.0).astype(jnp.bfloat16)
    grad_rows = jnp.where(keep_rows, cotangent.astype(jnp.float32), 0.0)
    d_gate_mlp = jnp.sum(grad_rows * mlp_out, axis=1)
    d_mlp = (gate_mlp * grad_rows).astype(jnp.bfloat16)
    d_mlp_all = lax.all_gather(d_mlp, "mp", axis=0, tiled=True)
    normed_again = lax.all_gather(normed_mlp, "mp", axis=0, tiled=True)
    pre_again = jnp.einsum("wtd,df->wtf", normed_again, w_up, preferred_element_type=jnp.float32)
    act_again = gelu_tanh(pre_again).astype(jnp.bfloat16)
    w_down_grad = jnp.einsum(
        "wtf,wtd->fd", act_again, d_mlp_all, preferred_element_type=jnp.float32
    )
    d_act = jnp.einsum("wtd,fd->wtf", d_mlp_all, w_down, preferred_element_type=jnp.float32)
    d_hidden = jax.vjp(gelu_tanh, pre_again)[1](d_act)[0].astype(jnp.bfloat16)
    w_up_grad = jnp.einsum(
        "wtd,wtf->df", normed_again, d_hidden, preferred_element_type=jnp.float32
    )
    row_block = d_hidden
    d_normed_mlp = lax.psum_scatter(
        jnp.einsum("wtf,df->wtd", row_block, w_up, preferred_element_type=jnp.float32),
        "mp",
        scatter_dimension=0,
        tiled=True,
    )
    pull_mlp = jax.vjp(modulate, middle, scale_mlp, shift_mlp)[1]
    d_middle_norm, d_scale_mlp, d_shift_mlp = pull_mlp(d_normed_mlp)
    d_middle = grad_rows + d_middle_norm
    d_gate_attn = jnp.sum(d_middle * branch, axis=1)
    d_branch = (gate_attn * d_middle).astype(jnp.bfloat16)
    d_branch_all = lax.all_gather(d_branch, "mp", axis=0, tiled=True)
    w_out_grad = jnp.einsum(
        "wte,wtd->ed", attended, d_branch_all, preferred_element_type=jnp.float32
    )
    d_attended = (
        jnp.einsum("wtd,ed->wte", d_branch_all, w_out, preferred_element_type=jnp.float32)
        .astype(jnp.bfloat16)
        .reshape(split_shape)
    )
    probs_back = jnp.exp(make_scores(queries, keys, rel_bias, keep_keys, score_scale) - log_total)
    d_probs = jnp.einsum("wihd,wjhd->whij", d_attended, values, preferred_element_type=jnp.float32)
    d_values = jnp.einsum(
        "whij,wihd->wjhd",
        probs_back.astype(jnp.bfloat16),
        d_attended,
        preferred_element_type=jnp.float32,
    ).astype(jnp.bfloat16)
    row_delta = jnp.sum(probs_back * d_probs, axis=-1, keepdims=True)
    d_scores = (probs_back * (d_probs - row_delta)).astype(jnp.bfloat16)
    d_queries = (
        jnp.einsum("whij,wjhd->wihd", d_scores, keys, preferred_element_type=jnp.float32)
        * score_scale
    ).astype(jnp.bfloat16)
    d_keys = (
        jnp.einsum("whij,wihd->wjhd", d_scores, queries, preferred_element_type=jnp.float32)
        * score_scale
    ).astype(jnp.bfloat16)
    d_bias = jnp.sum(d_scores, axis=0, dtype=jnp.float32).reshape(
        local_heads, WSIDE, WSIDE, WSIDE, WSIDE
    )
    d_half = jnp.einsum("hyxzw,bxw->hyzb", d_bias, offset_pick, precision=HIGH)
    rel_table_grad = jnp.einsum("hyzb,ayz->hab", d_half, offset_pick, precision=HIGH).reshape(
        local_heads, rel_span * rel_span
    )
    d_projected = jnp.stack([d_queries, d_keys, d_values]).reshape(
        3, group_size, win_tok, local_heads * HEAD_DIM
    )
    w_qkv_grad = jnp.einsum(
        "wtd,kwte->kde", gathered_attn, d_projected, preferred_element_type=jnp.float32
    )
    row_block = d_projected
    d_normed_attn = lax.psum_scatter(
        jnp.einsum("kwte,kde->wtd", row_block, w_qkv, preferred_element_type=jnp.float32).astype(
            jnp.bfloat16
        ),
        "mp",
        scatter_dimension=0,
        tiled=True,
    ).astype(jnp.float32)
    pull_attn = jax.vjp(modulate, inputs, scale_attn, shift_attn)[1]
    d_inputs_norm, d_scale_attn, d_shift_attn = pull_attn(d_normed_attn)
    tokens_grad = (d_middle + d_inputs_norm).astype(jnp.bfloat16)
    d_mod_own = jnp.stack(
        [
            d_shift_attn[:, 0],
            d_scale_attn[:, 0],
            d_gate_attn,
            d_shift_mlp[:, 0],
            d_scale_mlp[:, 0],
            d_gate_mlp,
        ],
        axis=1,
    ).reshape(own_count, 6 * width)
    d_modulation = lax.all_gather(d_mod_own.astype(jnp.bfloat16), "mp", axis=0, tiled=True).astype(
        d_mod_own.dtype
    )
    d_condition = exact(d_modulation, w_mod.T)
    d_cond_pre = jax.vjp(jax.nn.silu, cond_pre)[1](d_condition)[0]
    time_weight_grad = exact(features.astype(jnp.float32).T, d_cond_pre)
    class_table_grad = exact(onehot.astype(jnp.float32).T, d_cond_pre)
    w_mod_grad = exact(condition.astype(jnp.float32).T, d_modulation)
    b_mod_grad = jnp.sum(d_modulation, axis=0).reshape(6, width)
    (
        w_qkv_grad,
        w_out_grad,
        w_up_grad,
        w_down_grad,
        w_mod_grad,
        b_mod_grad,
        time_weight_grad,
        class_table_grad,
        rel_table_grad,
    ) = lax.psum(
        (
            w_qkv_grad,
            w_out_grad,
            w_up_grad,
            w_down_grad,
            w_mod_grad,
            b_mod_grad,
            time_weight_grad,
            class_table_grad,
            rel_table_grad,
        ),
        "dp",
    )
    return (
        block_out,
        tokens_grad,
        w_qkv_grad,
        w_out_grad,
        w_up_grad,
        w_down_grad,
        w_mod_grad,
        b_mod_grad,
        time_weight_grad,
        class_table_grad,
        rel_table_grad,
    )


def solution(mesh):
    return jax.shard_map(
        per_device,
        mesh=mesh,
        in_specs=(
            P(("dp", "mp"), None, None),
            P(("dp", "mp"), None, None),
            P(None, None, "mp"),
            P("mp", None),
            P(None, "mp"),
            P("mp", None),
            P("mp", None),
            P(),
            P(None, "mp"),
            P(None, "mp"),
            P("mp", None),
            P("dp"),
            P("dp"),
            P("dp"),
        ),
        out_specs=(
            P(("dp", "mp"), None, None),
            P(("dp", "mp"), None, None),
            P(None, None, "mp"),
            P("mp", None),
            P(None, "mp"),
            P("mp", None),
            P("mp", None),
            P(),
            P(None, "mp"),
            P(None, "mp"),
            P("mp", None),
        ),
        check_vma=False,
    )
```

profile of v0, /device:TPU:0, one launch (start us, length us, event | category | flops | bytes accessed | tf_op | source)
XLA Modules:
  0.0 1149.7 jit_solution(5632088591709699951)
XLA Ops:
  14.9 34.8 %all-reduce.5.cloned.1.call-done = f32[8,6,1024]{2,0,1:T(8,128)} async-done(((f32[8,6,1024]{2,0,1:T(8,128)}), f32[8,6,1024]{2,0,1:T(8,128)}) %all-reduce.5.cloned.1.call-update) | async-done | bytes 196624 | tf_op jit(solution)/shard_map/psum | solution.py:86
  54.1 5.6 convolution_bitcast_fusion
  59.8 12.0 %copy.103 = f32[4,16,16,16,16]{2,1,4,3,0:T(8,128)} copy(f32[4,16,16,16,16]{3,4,1,0,2:T(8,128)} %convolution_bitcast_fusion) | data formatting | bytes 2097152 | tf_op jit(solution)/shard_map/add | solution.py:49
  71.8 7.0 reshape.213
  78.9 55.0 %all-gather.6.cloned.1.call-done = bf16[8,256,1024]{2,1,0:T(8,128)(2,1)} async-done(((bf16[2,256,1024]{2,1,0:T(8,128)(2,1)}), bf16[8,256,1024]{2,1,0:T(8,128)(2,1)}) %all-gather.6.cloned.1.call-update) | async-done | bytes 4194320 | tf_op jit(solution)/shard_map/all_gather | solution.py:104
  133.9 6.1 convert_bitcast_fusion
  153.3 75.4 %reduce-scatter.5.cloned.1.call-done = bf16[2,256,1024]{2,1,0:T(8,128)(2,1)} async-done(((bf16[8,256,1024]{2,1,0:T(8,128)(2,1)}), bf16[2,256,1024]{2,1,0:T(8,128)(2,1)}) %reduce-scatter.5.cloned.1.call-update) | async-done | bytes 1048592 | tf_op jit(solution)/shard_map/reduce_scatter | solution.py:122
  237.2 78.7 %all-gather.8.cloned.1.call-done = bf16[8,256,1024]{2,1,0:T(8,128)(2,1)} async-done(((bf16[2,256,1024]{2,1,0:T(8,128)(2,1)}), bf16[8,256,1024]{2,1,0:T(8,128)(2,1)}) %all-gather.8.cloned.1.call-update) | async-done | bytes 4194320 | tf_op jit(solution)/shard_map/all_gather | solution.py:132
  316.0 10.9 fusion.34
  326.9 70.4 %all-gather.10.cloned.1.call-done = bf16[8,256,1024]{2,1,0:T(8,128)(2,1)} async-done(((bf16[2,256,1024]{2,1,0:T(8,128)(2,1)}), bf16[8,256,1024]{2,1,0:T(8,128)(2,1)}) %all-gather.10.cloned.1.call-update) | async-done | bytes 4194320 | tf_op jit(solution)/shard_map/all_gather | solution.py:148
  397.2 12.8 %fusion.6 = bf16[8,256,1024]{2,1,0:T(8,128)(2,1)S(1)} fusion(f32[8,256,1024]{2,1,0:T(8,128)} %fusion.34, bf16[8,256,1024]{2,1,0:T(8,128)(2,1)} %all-gather.10.cloned.1.call-done, bf16[1024,1024]{1,0:T(8,128)(2,1)} %param.19), kind=kOutput, calls=%fused_computation.8 | convolution fusion | flops 4336910336 | bytes 18874368 | tf_op jit(solution)/shard_map/wtd,fd->wtf/dot_general | solution.py:155
  412.0 7.0 fusion.32
  419.1 143.2 %reduce-scatter.9.cloned.1.call-done = f32[2,256,1024]{2,1,0:T(8,128)} async-done(((f32[8,256,1024]{2,1,0:T(8,128)}), f32[2,256,1024]{2,1,0:T(8,128)}) %reduce-scatter.9.cloned.1.call-update) | async-done | bytes 2097168 | tf_op jit(solution)/shard_map/reduce_scatter | solution.py:161
  569.6 81.5 %all-gather.12.cloned.1.call-done = bf16[8,256,1024]{2,1,0:T(8,128)(2,1)} async-done(((bf16[2,256,1024]{2,1,0:T(8,128)(2,1)}), bf16[8,256,1024]{2,1,0:T(8,128)(2,1)}) %all-gather.12.cloned.1.call-update) | async-done | bytes 4194320 | tf_op jit(solution)/shard_map/all_gather | solution.py:172
  651.0 3.7 convolution_convert_fusion.3
  654.8 6.0 convolution_convert_fusion.2
  663.3 3.9 convert_reduce_fusion
  678.1 7.8 bitcast_convert_fusion
  686.0 11.5 %convolution_convert_fusion = bf16[8,256,1024]{2,1,0:T(8,128)(2,1)} fusion(bf16[1024,1024]{1,0:T(8,128)(2,1)} %param.19, f32[8,256,1024]{2,1,0:T(8,128)} %fusion.34), kind=kOutput, calls=%fused_computation.34 | convolution fusion | flops 4315938816 | bytes 14680064 | tf_op jit(solution)/shard_map/wtf,fd->wtd/dot_general | solution.py:137
  697.8 10.2 convolution_bitcast_fusion.2
  708.1 11.2 convolution_bitcast_fusion.1
  722.8 5.5 fusion.36
  728.3 33.1 %reduce-scatter.11.cloned.1.call-done = bf16[2,256,1024]{2,1,0:T(8,128)(2,1)} async-done(((bf16[8,256,1024]{2,1,0:T(8,128)(2,1)}), bf16[2,256,1024]{2,1,0:T(8,128)(2,1)}) %reduce-scatter.11.cloned.1.call-update) | async-done | bytes 1048592 | tf_op jit(solution)/shard_map/reduce_scatter | solution.py:213
  767.7 74.0 %reduce-scatter.7.cloned.1.call-done = bf16[2,256,1024]{2,1,0:T(8,128)(2,1)} async-done(((bf16[8,256,1024]{2,1,0:T(8,128)(2,1)}), bf16[2,256,1024]{2,1,0:T(8,128)(2,1)}) %reduce-scatter.7.cloned.1.call-update) | async-done | bytes 1048592 | tf_op jit(solution)/shard_map/reduce_scatter | solution.py:136
  841.6 5.2 fusion.26
  847.0 13.8 %all-gather = bf16[4,2,6144]{2,1,0:T(2,128)(2,1)S(1)} all-gather(bf16[1,2,6144]{2,1,0:T(2,128)(2,1)S(1)} %bitcast.178), channel_id=1, replica_groups=mesh['dp'=8,'mp'=4] {'mp'}, dimensions={0}, use_global_device_ids=true | all-gather | bytes 122880 | tf_op jit(solution)/shard_map/all_gather | solution.py:235
  864.4 3.7 fusion.77
  869.0 6.2 reshape.189
  875.2 6.8 convolution_bitcast_fusion.5
  882.7 25.6 %all-reduce = (f32[6,1024]{1,0:T(8,128)}, f32[4,961]{1,0:T(4,128)}) all-reduce(f32[6,1024]{1,0:T(8,128)S(1)} %reshape.188, f32[4,961]{1,0:T(4,128)S(1)} %reshape.190), channel_id=1, replica_groups=mesh['dp'=8,'mp'=4] {'dp'}, use_global_device_ids=true, to_apply=%region_28.29 | all-reduce | flops 9988 | bytes 79904 | tf_op jit(solution)/shard_map/psum | solution.py:254
  908.3 215.6 %all-reduce.7.cloned.1.call-done = (f32[3,1024,256]{1,2,0:T(8,128)}, f32[256,1024]{1,0:T(8,128)}, f32[1024,1024]{1,0:T(8,128)}, f32[1024,1024]{1,0:T(8,128)}, f3...) async-done(((f32[3,1024,256]{1,2,0:T(8,128)}, f32[256,1024]{1,0:T(8,128)}, f32[1024,1024]{1,0:T(8,128)}, f32[1024,1024]{1,0:T(8,128)}, ...) | async-done | bytes 20160528 | tf_op jit(solution)/shard_map/psum | solution.py:254
  1129.7 5.1 copy.125
  (172 shorter events, 85.5 us)
Async XLA Ops:
  7.2 42.5 %all-reduce.5.cloned.1.call-start = ((), (), s32[]{:S(2)}) async-start(), calls=%async_computation.4 | async-start | bytes 393216 | tf_op jit(solution)/shard_map/psum | solution.py:86
  8.2 6.7 copy-start.27
  11.7 41.7 %copy-start.28 = (bf16[4,961]{1,0:T(4,128)(2,1)S(1)}, bf16[4,961]{1,0:T(4,128)(2,1)}, u32[]{:S(2)}) copy-start(bf16[4,961]{1,0:T(4,128)(2,1)} %param.24) | copy-start | bytes 23068
  11.7 122.2 %all-gather.6.cloned.1.call-start = ((), (), s32[]{:S(2)}) async-start(), calls=%async_computation.5 | async-start | bytes 5242880 | tf_op jit(solution)/shard_map/all_gather | solution.py:104
  53.3 175.4 %reduce-scatter.5.cloned.1.call-start = ((), (), s32[]{:S(2)}) async-start(), calls=%async_computation.6 | async-start | bytes 5242880 | tf_op jit(solution)/shard_map/reduce_scatter | solution.py:122
  71.8 7.0 copy-start.30
  140.3 4.0 copy-start.7
  140.3 4.0 copy-start.12
  140.3 5.7 copy-start.9
  153.3 162.7 %all-gather.8.cloned.1.call-start = ((), (), s32[]{:S(2)}) async-start(), calls=%async_computation.7 | async-start | bytes 5242880 | tf_op jit(solution)/shard_map/all_gather | solution.py:132
  228.7 4.2 copy-start.2
  228.7 4.2 copy-start.4
  234.6 162.6 %all-gather.10.cloned.1.call-start = ((), (), s32[]{:S(2)}) async-start(), calls=%async_computation.9 | async-start | bytes 5242880 | tf_op jit(solution)/shard_map/all_gather | solution.py:148
  237.2 325.1 %reduce-scatter.9.cloned.1.call-start = ((), (), s32[]{:S(2)}) async-start(), calls=%async_computation.10 | async-start | bytes 10485760 | tf_op jit(solution)/shard_map/reduce_scatter | solution.py:161
  397.2 14.8 %copy-start.34 = (bf16[1024,1024]{1,0:T(8,128)(2,1)S(1)}, bf16[1024,1024]{1,0:T(8,128)(2,1)}, u32[]{:S(2)}) copy-start(bf16[1024,1024]{1,0:T(8,128)(2,1)} %param.18) | copy-start | bytes 6291460
  419.0 232.0 %all-gather.12.cloned.1.call-start = ((), (), s32[]{:S(2)}) async-start(), calls=%async_computation.11 | async-start | bytes 5242880 | tf_op jit(solution)/shard_map/all_gather | solution.py:172
  562.3 3.5 copy-start.14
  569.5 191.9 %reduce-scatter.11.cloned.1.call-start = ((), (), s32[]{:S(2)}) async-start(), calls=%async_computation.12 | async-start | bytes 5242880 | tf_op jit(solution)/shard_map/reduce_scatter | solution.py:213
  651.0 9.7 slice-start
  654.8 6.0 slice-start.1
  654.8 6.0 copy-start.10
  663.3 3.9 copy-start.13
  686.0 155.7 %reduce-scatter.7.cloned.1.call-start = ((), (), s32[]{:S(2)}) async-start(), calls=%async_computation.8 | async-start | bytes 5242880 | tf_op jit(solution)/shard_map/reduce_scatter | solution.py:136
  697.6 426.2 %all-reduce.7.cloned.1.call-start = ((), (), s32[]{:S(2)}) async-start(), calls=%async_computation.13 | async-start | bytes 40321024 | tf_op jit(solution)/shard_map/psum | solution.py:254
  697.8 10.2 copy-start.32
  708.1 11.2 copy-start.18
  708.1 11.2 copy-start.33
  719.3 3.6 copy-start.31
  846.9 15.9 %copy-start.29 = (s32[8]{0:T(128)S(1)}, s32[8]{0:T(128)}, u32[]{:S(2)}) copy-start(s32[8]{0:T(128)} %param.26) | copy-start | bytes 100
  1129.7 5.1 copy-start.16
  1129.7 7.2 slice-start.2
  1134.8 3.5 slice-start.3
  (18 other events, 40.4 us)
Sparse Core Ops, SparseCore 0:
  11.9 37.7 all-reduce.4
  53.5 80.3 all-gather.5
  153.4 75.2 reduce-scatter.4
  234.7 81.2 all-gather.7
  318.0 79.2 all-gather.9
  419.2 143.0 reduce-scatter.8
  569.6 81.3 all-gather.11
  686.1 75.2 reduce-scatter.10
  764.3 77.2 reduce-scatter.6
  868.3 255.4 all-reduce.6
where the time goes:
time: 1160 us; the launch traced here: 1150 us
  waiting for transfers between devices  862 us (74%)
  matrix products  133 us (11%)
  local copies, waits for them, and re-layouts  60.8 us (5%)
  blocking collectives  39.4 us (3%)
  other arithmetic  38.9 us (3%)
  between operations  14.9 us (1%)
    psum x1, waiting for transfers between devices, per_device(): lax.psum((w_qkv_grad, w_out_grad, w_up_grad, w_down_grad, w_mod_grad, b_m...  216 us
    reduce_scatter x1, waiting for transfers between devices, per_device(): lax.psum_scatter(jnp.einsum('wtf,df->wtd', row_block, w_up, preferred_ele...  143 us
    all_gather x1, waiting for transfers between devices, per_device(): d_branch_all = lax.all_gather(d_branch, 'mp', axis=0, tiled=True)  81.5 us
    all_gather x1, waiting for transfers between devices, per_device(): gathered_mlp = lax.all_gather(normed_mlp, 'mp', axis=0, tiled=True)  78.7 us
    reduce_scatter x1, waiting for transfers between devices, per_device(): lax.psum_scatter(jnp.einsum('wte,ed->wtd', row_block, w_out, preferred_el...  75.4 us
    reduce_scatter x1, waiting for transfers between devices, per_device(): lax.psum_scatter(jnp.einsum('wtf,fd->wtd', row_block, w_down, preferred_e...  74 us
    all_gather x1, waiting for transfers between devices, per_device(): d_mlp_all = lax.all_gather(d_mlp, 'mp', axis=0, tiled=True)  70.4 us
    all_gather x1, waiting for transfers between devices, per_device(): gathered_attn = lax.all_gather(normed_attn, 'mp', axis=0, tiled=True)  55 us
  transfers between devices with their start and end apart: 10, of which 10 were waited for; matrix products, arithmetic and copies ran while one was open for 9% of the time, Pallas kernels for 0%

commit v1 on v0

--- a/solution.py
+++ b/solution.py
@@ -1,3 +1,4 @@
+import functools
 import math
 import jax
 import jax.numpy as jnp
@@ -10,6 +11,21 @@
 EPS = 1e-06
 HIGH = lax.Precision.HIGHEST
 MASKED = -1000000000.0
+
+
+def _detail_block(body, device_axis):
+    tmp, step_out = (jax.lax.axis_size(device_axis), jax.lax.axis_index(device_axis))
+    side_arr, heard = (body, 1)
+    while heard < tmp:
+        t1 = jax.lax.ppermute(side_arr, device_axis, [(ix, ix ^ heard) for ix in range(tmp)])
+        z1 = jnp.concatenate([side_arr, t1], axis=0)
+        block_now = jnp.concatenate([t1, side_arr], axis=0)
+        side_arr = jnp.where(step_out & heard == 0, z1, block_now)
+        heard = 2 * heard
+    return side_arr
+
+
+work_pipes_up = functools.partial(_detail_block, device_axis="mp")
 
 
 def exact(matrix_a, matrix_b):
@@ -101,7 +117,7 @@
     )
     inputs = tokens.astype(jnp.float32)
     normed_attn = modulate(inputs, scale_attn, shift_attn).astype(jnp.bfloat16)
-    gathered_attn = lax.all_gather(normed_attn, "mp", axis=0, tiled=True)
+    gathered_attn = work_pipes_up(normed_attn)
     projected = jnp.einsum(
         "wtd,kde->kwte", gathered_attn, w_qkv, preferred_element_type=jnp.float32
     ).astype(jnp.bfloat16)

time: 1160 us -> 1200 us (1.034)
  waiting for transfers between devices: 862 us -> 890 us
    ppermute x0 -> x2, waiting for transfers between devices: none -> 84.6 us  [_detail_block(): jax.lax.ppermute(side_arr, device_axis, [(ix, ix ^ heard) for ix in range...]
    all_gather x1 -> x0, waiting for transfers between devices: 55 us -> none  [per_device(): gathered_attn = lax.all_gather(normed_attn, 'mp', axis=0, tiled=True)]
    unnamed x93 -> x111, local copies, waits for them, and re-layouts: 28.4 us -> 27.8 us
  transfers between devices with their start and end apart: 10 -> 11, of which waited for: 10 -> 11; matrix products, arithmetic and copies ran while one was open for 9% -> 9% of each run, Pallas kernels for 0% -> 0%
where the time goes in v1:
time: 1200 us; the launch traced here: 1190 us
  waiting for transfers between devices  890 us (74%)
  matrix products  138 us (12%)
  local copies, waits for them, and re-layouts  60.1 us (5%)
  other arithmetic  42.9 us (4%)
  blocking collectives  39.5 us (3%)
  between operations  14.8 us (1%)
    psum x1, waiting for transfers between devices, per_device(): lax.psum((w_qkv_grad, w_out_grad, w_up_grad, w_down_grad, w_mod_grad, b_m...  215 us
    reduce_scatter x1, waiting for transfers between devices, per_device(): lax.psum_scatter(jnp.einsum('wtf,df->wtd', row_block, w_up, preferred_ele...  143 us
    ppermute x2, waiting for transfers between devices, _detail_block(): jax.lax.ppermute(side_arr, device_axis, [(ix, ix ^ heard) for ix in range...  84.6 us
    all_gather x1, waiting for transfers between devices, per_device(): d_branch_all = lax.all_gather(d_branch, 'mp', axis=0, tiled=True)  81.5 us
    all_gather x1, waiting for transfers between devices, per_device(): gathered_mlp = lax.all_gather(normed_mlp, 'mp', axis=0, tiled=True)  78.8 us
    reduce_scatter x1, waiting for transfers between devices, per_device(): lax.psum_scatter(jnp.einsum('wte,ed->wtd', row_block, w_out, preferred_el...  76.9 us
    reduce_scatter x1, waiting for transfers between devices, per_device(): lax.psum_scatter(jnp.einsum('wtf,fd->wtd', row_block, w_down, preferred_e...  73.9 us
    all_gather x1, waiting for transfers between devices, per_device(): d_mlp_all = lax.all_gather(d_mlp, 'mp', axis=0, tiled=True)  70.4 us
  transfers between devices with their start and end apart: 11, of which 11 were waited for; matrix products, arithmetic and copies ran while one was open for 9% of the time, Pallas kernels for 0%

profile of v1, /device:TPU:0, one launch (start us, length us, event | category | flops | bytes accessed | tf_op | source)
XLA Modules:
  0.0 1189.9 jit_solution(5076066841870720347)
XLA Ops:
  15.6 34.7 %all-reduce.5.cloned.1.call-done = f32[8,6,1024]{2,0,1:T(8,128)} async-done(((f32[8,6,1024]{2,0,1:T(8,128)}), f32[8,6,1024]{2,0,1:T(8,128)}) %all-reduce.5.cloned.1.call-update) | async-done | bytes 196624 | tf_op jit(solution)/shard_map/psum | solution.py:102
  55.3 21.7 %collective-permute-done = bf16[2,256,1024]{2,1,0:T(8,128)(2,1)} collective-permute-done((bf16[2,256,1024]{2,1,0:T(8,128)(2,1)}, bf16[2,256,1024]{2,1,0:T(8,128)(2,1)}, u32[]{:S(2)}, u32[]{:S(2)}) %collective-permute-start) | collective-permute-done | bytes 1048608 | tf_op jit(solution)/shard_map/ppermute | solution.py:20
  77.0 3.9 maximum_select_fusion.1
  84.0 5.7 convolution_bitcast_fusion
  89.6 11.9 %copy.103 = f32[4,16,16,16,16]{2,1,4,3,0:T(8,128)} copy(f32[4,16,16,16,16]{3,4,1,0,2:T(8,128)} %convolution_bitcast_fusion) | data formatting | bytes 2097152 | tf_op jit(solution)/shard_map/add | solution.py:65
  101.5 6.9 reshape.213
  108.6 62.9 %collective-permute-done.1 = bf16[4,256,1024]{2,1,0:T(8,128)(2,1)} collective-permute-done((bf16[4,256,1024]{2,1,0:T(8,128)(2,1)}, bf16[4,256,1024]{2,1,0:T(8,128)(2,1)}, u32[]{:S(2)}, u32[]{:S(2)}) %collective-permute-start.1) | collective-permute-done | bytes 2097184 | tf_op jit(solution)/shard_map/ppermute | solution.py:20
  171.5 7.4 convert_bitcast_fusion
  192.1 76.9 %reduce-scatter.5.cloned.1.call-done = bf16[2,256,1024]{2,1,0:T(8,128)(2,1)} async-done(((bf16[8,256,1024]{2,1,0:T(8,128)(2,1)}), bf16[2,256,1024]{2,1,0:T(8,128)(2,1)}) %reduce-scatter.5.cloned.1.call-update) | async-done | bytes 1048592 | tf_op jit(solution)/shard_map/reduce_scatter | solution.py:138
  277.6 78.8 %all-gather.5.cloned.1.call-done = bf16[8,256,1024]{2,1,0:T(8,128)(2,1)} async-done(((bf16[2,256,1024]{2,1,0:T(8,128)(2,1)}), bf16[8,256,1024]{2,1,0:T(8,128)(2,1)}) %all-gather.5.cloned.1.call-update) | async-done | bytes 4194320 | tf_op jit(solution)/shard_map/all_gather | solution.py:148
  356.3 10.9 fusion.35
  367.2 70.4 %all-gather.7.cloned.1.call-done = bf16[8,256,1024]{2,1,0:T(8,128)(2,1)} async-done(((bf16[2,256,1024]{2,1,0:T(8,128)(2,1)}), bf16[8,256,1024]{2,1,0:T(8,128)(2,1)}) %all-gather.7.cloned.1.call-update) | async-done | bytes 4194320 | tf_op jit(solution)/shard_map/all_gather | solution.py:164
  437.6 12.7 %fusion.6 = bf16[8,256,1024]{2,1,0:T(8,128)(2,1)S(1)} fusion(f32[8,256,1024]{2,1,0:T(8,128)} %fusion.35, bf16[8,256,1024]{2,1,0:T(8,128)(2,1)} %all-gather.7.cloned.1.call-done, bf16[1024,1024]{1,0:T(8,128)(2,1)} %param.19), kind=kOutput, calls=%fused_computation.8 | convolution fusion | flops 4336910336 | bytes 18874368 | tf_op jit(solution)/shard_map/wtd,fd->wtf/dot_general | solution.py:171
  452.4 7.0 fusion.33
  459.4 143.2 %reduce-scatter.9.cloned.1.call-done = f32[2,256,1024]{2,1,0:T(8,128)} async-done(((f32[8,256,1024]{2,1,0:T(8,128)}), f32[2,256,1024]{2,1,0:T(8,128)}) %reduce-scatter.9.cloned.1.call-update) | async-done | bytes 2097168 | tf_op jit(solution)/shard_map/reduce_scatter | solution.py:177
  609.9 81.5 %all-gather.9.cloned.1.call-done = bf16[8,256,1024]{2,1,0:T(8,128)(2,1)} async-done(((bf16[2,256,1024]{2,1,0:T(8,128)(2,1)}), bf16[8,256,1024]{2,1,0:T(8,128)(2,1)}) %all-gather.9.cloned.1.call-update) | async-done | bytes 4194320 | tf_op jit(solution)/shard_map/all_gather | solution.py:188
  695.1 6.0 convolution_convert_fusion.2
  703.6 3.9 convert_reduce_fusion
  718.5 7.8 bitcast_convert_fusion
  726.4 11.5 convolution_convert_fusion
  738.2 10.2 convolution_bitcast_fusion.2
  748.4 11.2 convolution_bitcast_fusion.1
  761.9 8.9 fusion.37
  770.9 30.9 %reduce-scatter.11.cloned.1.call-done = bf16[2,256,1024]{2,1,0:T(8,128)(2,1)} async-done(((bf16[8,256,1024]{2,1,0:T(8,128)(2,1)}), bf16[2,256,1024]{2,1,0:T(8,128)(2,1)}) %reduce-scatter.11.cloned.1.call-update) | async-done | bytes 1048592 | tf_op jit(solution)/shard_map/reduce_scatter | solution.py:229
  808.1 73.9 %reduce-scatter.7.cloned.1.call-done = bf16[2,256,1024]{2,1,0:T(8,128)(2,1)} async-done(((bf16[8,256,1024]{2,1,0:T(8,128)(2,1)}), bf16[2,256,1024]{2,1,0:T(8,128)(2,1)}) %reduce-scatter.7.cloned.1.call-update) | async-done | bytes 1048592 | tf_op jit(solution)/shard_map/reduce_scatter | solution.py:152
  882.0 5.2 fusion.27
  887.3 13.8 %all-gather = bf16[4,2,6144]{2,1,0:T(2,128)(2,1)S(1)} all-gather(bf16[1,2,6144]{2,1,0:T(2,128)(2,1)S(1)} %bitcast.177), channel_id=1, replica_groups=mesh['dp'=8,'mp'=4] {'mp'}, dimensions={0}, use_global_device_ids=true | all-gather | bytes 122880 | tf_op jit(solution)/shard_map/all_gather | solution.py:251
  909.4 6.2 reshape.189
  915.6 6.8 convolution_bitcast_fusion.5
  923.1 25.7 %all-reduce = (f32[6,1024]{1,0:T(8,128)}, f32[4,961]{1,0:T(4,128)}) all-reduce(f32[6,1024]{1,0:T(8,128)S(1)} %reshape.188, f32[4,961]{1,0:T(4,128)S(1)} %reshape.190), channel_id=1, replica_groups=mesh['dp'=8,'mp'=4] {'dp'}, use_global_device_ids=true, to_apply=%region_28.29 | all-reduce | flops 9988 | bytes 79904 | tf_op jit(solution)/shard_map/psum | solution.py:270
  948.8 215.4 %all-reduce.7.cloned.1.call-done = (f32[3,1024,256]{1,2,0:T(8,128)}, f32[256,1024]{1,0:T(8,128)}, f32[1024,1024]{1,0:T(8,128)}, f32[1024,1024]{1,0:T(8,128)}, f3...) async-done(((f32[3,1024,256]{1,2,0:T(8,128)}, f32[256,1024]{1,0:T(8,128)}, f32[1024,1024]{1,0:T(8,128)}, f32[1024,1024]{1,0:T(8,128)}, ...) | async-done | bytes 20160528 | tf_op jit(solution)/shard_map/psum | solution.py:270
  1170.1 5.1 copy.125
  (192 shorter events, 96.0 us)
Async XLA Ops:
  7.2 43.1 %all-reduce.5.cloned.1.call-start = ((), (), s32[]{:S(2)}) async-start(), calls=%async_computation.4 | async-start | bytes 393216 | tf_op jit(solution)/shard_map/psum | solution.py:102
  8.2 7.3 copy-start.37
  12.4 256.7 %reduce-scatter.5.cloned.1.call-start = ((), (), s32[]{:S(2)}) async-start(), calls=%async_computation.5 | async-start | bytes 5242880 | tf_op jit(solution)/shard_map/reduce_scatter | solution.py:138
  15.5 34.8 %copy-start.35 = (f32[2,256]{1,0:T(2,128)}, f32[2,256]{1,0:T(2,128)S(1)}, u32[]{:S(2)}) copy-start(f32[2,256]{1,0:T(2,128)S(1)} %fusion.29) | copy-start | bytes 6148
  15.6 65.4 %copy-start.29 = (f32[2,256]{1,0:T(2,128)}, f32[2,256]{1,0:T(2,128)S(1)}, u32[]{:S(2)}) copy-start(f32[2,256]{1,0:T(2,128)S(1)} %fusion.72) | copy-start | bytes 6148
  51.3 31.9 %copy-start.38 = (bf16[4,961]{1,0:T(4,128)(2,1)S(1)}, bf16[4,961]{1,0:T(4,128)(2,1)}, u32[]{:S(2)}) copy-start(bf16[4,961]{1,0:T(4,128)(2,1)} %param.24) | copy-start | bytes 23068
  54.0 23.1 %collective-permute-start = (bf16[2,256,1024]{2,1,0:T(8,128)(2,1)}, bf16[2,256,1024]{2,1,0:T(8,128)(2,1)}, u32[]{:S(2)}, u32[]{:S(2)}) collective-permute-start(bf16[2,256,1024]{2,1,0:T(8,128)(2,1)} %fusion.22), channel_id=1, source_target_pairs={{0,1},{1,0},{2,3},{3,2},{4,5},{5,4},{6,7},{7,6},{8,9},{9,8},{10,11... | collective-permute-start | bytes 3145736 | tf_op jit(solution)/shard_map/ppermute | solution.py:20
  81.0 90.5 %collective-permute-start.1 = (bf16[4,256,1024]{2,1,0:T(8,128)(2,1)}, bf16[4,256,1024]{2,1,0:T(8,128)(2,1)}, u32[]{:S(2)}, u32[]{:S(2)}) collective-permute-start(bf16[4,256,1024]{2,1,0:T(8,128)(2,1)} %maximum_select_fusion.1), channel_id=1, source_target_pairs={{0,2},{1,3},{2,0},{3,1},{4,6},{5,7},{6,4},{7,5},{8,10},{9,11},{10,... | collective-permute-start | bytes 6291464 | tf_op jit(solution)/shard_map/ppermute | solution.py:20
  101.5 6.9 copy-start.40
  179.1 5.7 copy-start.9
  192.1 164.3 %all-gather.5.cloned.1.call-start = ((), (), s32[]{:S(2)}) async-start(), calls=%async_computation.6 | async-start | bytes 5242880 | tf_op jit(solution)/shard_map/all_gather | solution.py:148
  274.9 162.7 %all-gather.7.cloned.1.call-start = ((), (), s32[]{:S(2)}) async-start(), calls=%async_computation.8 | async-start | bytes 5242880 | tf_op jit(solution)/shard_map/all_gather | solution.py:164
  277.5 325.1 %reduce-scatter.9.cloned.1.call-start = ((), (), s32[]{:S(2)}) async-start(), calls=%async_computation.9 | async-start | bytes 10485760 | tf_op jit(solution)/shard_map/reduce_scatter | solution.py:177
  437.6 14.8 %copy-start.43 = (bf16[1024,1024]{1,0:T(8,128)(2,1)S(1)}, bf16[1024,1024]{1,0:T(8,128)(2,1)}, u32[]{:S(2)}) copy-start(bf16[1024,1024]{1,0:T(8,128)(2,1)} %param.18) | copy-start | bytes 6291460
  459.4 232.0 %all-gather.9.cloned.1.call-start = ((), (), s32[]{:S(2)}) async-start(), calls=%async_computation.10 | async-start | bytes 5242880 | tf_op jit(solution)/shard_map/all_gather | solution.py:188
  609.9 191.9 %reduce-scatter.11.cloned.1.call-start = ((), (), s32[]{:S(2)}) async-start(), calls=%async_computation.11 | async-start | bytes 5242880 | tf_op jit(solution)/shard_map/reduce_scatter | solution.py:229
  691.4 9.7 slice-start
  695.1 6.0 slice-start.1
  695.1 6.0 copy-start.10
  726.4 155.6 %reduce-scatter.7.cloned.1.call-start = ((), (), s32[]{:S(2)}) async-start(), calls=%async_computation.7 | async-start | bytes 5242880 | tf_op jit(solution)/shard_map/reduce_scatter | solution.py:152
  738.0 426.3 %all-reduce.7.cloned.1.call-start = ((), (), s32[]{:S(2)}) async-start(), calls=%async_computation.12 | async-start | bytes 40321024 | tf_op jit(solution)/shard_map/psum | solution.py:270
  738.2 10.2 copy-start.41
  748.4 11.2 copy-start.18
  748.4 11.2 copy-start.42
  770.9 34.5 %copy-start.36 = (f32[2,256]{1,0:T(2,128)S(1)}, f32[2,256]{1,0:T(2,128)}, u32[]{:S(2)}) copy-start(f32[2,256]{1,0:T(2,128)} %copy-done.35) | copy-start | bytes 6148
  770.9 34.5 %copy-start.30 = (f32[2,256]{1,0:T(2,128)S(1)}, f32[2,256]{1,0:T(2,128)}, u32[]{:S(2)}) copy-start(f32[2,256]{1,0:T(2,128)} %copy-done.29) | copy-start | bytes 6148
  887.2 14.9 %copy-start.28 = (f32[8,256]{1,0:T(8,128)S(1)}, f32[8,256]{1,0:T(8,128)}, u32[]{:S(2)}) copy-start(f32[8,256]{1,0:T(8,128)} %copy-done.27) | copy-start | bytes 24580
  887.2 14.9 %copy-start.32 = (bf16[8,128]{1,0:T(8,128)(2,1)S(1)}, bf16[8,128]{1,0:T(8,128)(2,1)}, u32[]{:S(2)}) copy-start(bf16[8,128]{1,0:T(8,128)(2,1)} %copy-done.31) | copy-start | bytes 6148
  887.2 14.9 %copy-start.34 = (bf16[8,128]{1,0:T(8,128)(2,1)S(1)}, bf16[8,128]{1,0:T(8,128)(2,1)}, u32[]{:S(2)}) copy-start(bf16[8,128]{1,0:T(8,128)(2,1)} %copy-done.33) | copy-start | bytes 6148
  887.3 15.9 %copy-start.39 = (s32[8]{0:T(128)S(1)}, s32[8]{0:T(128)}, u32[]{:S(2)}) copy-start(s32[8]{0:T(128)} %param.26) | copy-start | bytes 100
  1170.1 5.1 copy-start.16
  1170.1 7.2 slice-start.2
  (28 other events, 71.6 us)
Sparse Core Ops, SparseCore 0:
  12.5 37.7 all-reduce.4
  192.2 76.7 reduce-scatter.4
  275.0 81.2 all-gather.4
  358.3 79.2 all-gather.6
  459.5 143.0 reduce-scatter.8
  610.0 81.3 all-gather.8
  726.5 75.2 reduce-scatter.10
  804.7 77.2 reduce-scatter.6
  908.7 255.4 all-reduce.6
